TPU v7x, 32 devices: a whole 2x2x4 slice. The times are simulated.
32 devices in a mesh: grp: 2 (over x), seq: 16 (over z, y, core).
Axes of the slice: x: 2, y: 2, z: 4, core: 2. Of those that a mesh axis runs over, the one named last changes fastest.
Arguments:
- queries: bfloat16 [8192, 8192], P(('grp', 'seq')), parts along dimension 0, may hold values from -6 to 6
- keys_in: bfloat16 [8192, 8192], P(('grp', 'seq')), parts along dimension 0, may hold values from -0.375 to 0.375
- values_in: bfloat16 [8192, 8192], P(('grp', 'seq')), parts along dimension 0, may hold values from -6 to 6
- log_decay: bfloat16 [8192, 64], P(('grp', 'seq')), parts along dimension 0, may hold values from -2 to 0, as said below
- gate_logits: bfloat16 [8192, 8192], P(('grp', 'seq')), parts along dimension 0, may hold values from -6 to 6
- norm_gain: float32 [8192], replicated, may hold values from 0.1 to 1.9
- doc_lengths: int32 [16], P('grp'), parts along dimension 0, may hold values from 1 to 2048, 4096 in all
Outputs:
- attended: bfloat16 [8192, 8192], P(('grp', 'seq')), parts along dimension 0
- final_state: float32 [128, 128, 128], P(('grp', 'seq')), parts along dimension 0
There are 2 independent parts, one for each index of `grp`. A program takes and returns all parts, laid end to end along the dimension named above; an argument that names none is the same for every part. Nothing has to cross between parts.
Inputs may be any that keep to these rules, and one draw needn't show every extreme that they name: log_decay is negative. `doc_lengths`: the 8 lengths are positive and sum to 4096.
All inputs are finite; a program needn't handle non-finite values.
Results may differ from a plain program's by a relative error of at most 0.0049.
Values may be sent and summed in bfloat16 or wider, within the bound.
A program may use at most 320 MiB of HBM per device.

v0:
```python
import math
import jax
import jax.numpy as jnp
from jax import lax
from jax.sharding import PartitionSpec as P

HEADS = 64
HEAD_DIM = 128
SPAN = 256
EPS = 1e-05


def doc_index(doc_lengths, positions):
    doc_ends = jnp.cumsum(doc_lengths)
    return jnp.sum((positions[:, None] >= doc_ends[None, :]).astype(jnp.int32), axis=1)


def local_terms(query_blk, key_blk, value_blk, decay_blk, doc_blk, prior_doc):
    length = query_blk.shape[1]
    row_index = lax.broadcasted_iota(jnp.int32, (length, length), 0)
    col_index = lax.broadcasted_iota(jnp.int32, (length, length), 1)
    causal = row_index >= col_index
    cumulative = jnp.einsum(
        "ij,gjh->gih", causal.astype(jnp.float32), decay_blk, precision=lax.Precision.HIGHEST
    )
    allowed = causal[None] & (doc_blk[:, :, None] == doc_blk[:, None, :])
    cumul_heads = jnp.swapaxes(cumulative, 1, 2)
    spread_log = jnp.where(
        allowed[:, None], cumul_heads[:, :, :, None] - cumul_heads[:, :, None, :], 0.0
    )
    decay_grid = jnp.where(allowed[:, None], jnp.exp(spread_log), 0.0)
    scores = jnp.einsum("gihd,gjhd->ghij", query_blk, key_blk, preferred_element_type=jnp.float32)
    weights = (scores * decay_grid).astype(jnp.bfloat16)
    inside = jnp.einsum("ghij,gjhd->gihd", weights, value_blk, preferred_element_type=jnp.float32)
    carried = (doc_blk == prior_doc[:, None]).astype(jnp.float32)
    leading = carried[:, :, None] * jnp.exp(cumulative)
    closing_doc = (doc_blk == doc_blk[:, -1:]).astype(jnp.float32)
    key_weight = closing_doc[:, :, None] * jnp.exp(cumulative[:, -1:, :] - cumulative)
    weighted = (key_blk.astype(jnp.float32) * key_weight[..., None]).astype(jnp.bfloat16)
    update = jnp.einsum("gjhd,gjhe->ghde", weighted, value_blk, preferred_element_type=jnp.float32)
    factor = carried[:, -1:] * jnp.exp(cumulative[:, -1, :])
    return (inside, leading, factor, update)


def span_pass(query_rows, key_rows, value_rows, decay_rows, documents, before):
    spans = query_rows.shape[0]
    per_step = math.gcd(spans, max(1, 32 // query_rows.shape[2]))

    def blocked(array):
        return array.reshape((spans // per_step, per_step) + array.shape[1:])

    pieces = lax.map(
        lambda batch_item: local_terms(*batch_item),
        tuple(
            (
                blocked(array)
                for array in (query_rows, key_rows, value_rows, decay_rows, documents, before)
            )
        ),
    )
    return tuple((array.reshape((spans,) + array.shape[2:]) for array in pieces))


def join_states(first_pair, second_pair):
    return (
        first_pair[0] * second_pair[0],
        second_pair[0][..., None, None] * first_pair[1] + second_pair[1],
    )


def prefix_states(factor, update):
    running_factor, running_update = lax.associative_scan(join_states, (factor, update), axis=0)
    prior_factor = jnp.concatenate([jnp.ones_like(factor[:1]), running_factor[:-1]], axis=0)
    prior_update = jnp.concatenate([jnp.zeros_like(update[:1]), running_update[:-1]], axis=0)
    return (prior_factor, prior_update, running_factor[-1], running_update[-1])


def with_state(query_rows, inside, leading, states):
    across = jnp.einsum(
        "nihd,nhde->nihe", query_rows.astype(jnp.float32), states, precision=lax.Precision.HIGHEST
    )
    return inside + across * leading[..., None]


def shards(queries, keys_in, values_in, log_decay, gate_logits, norm_gain, doc_lengths):
    local_len = queries.shape[0]
    spans = local_len // SPAN
    positions = lax.axis_index("seq") * local_len + lax.iota(jnp.int32, local_len)
    documents = doc_index(doc_lengths, positions).reshape(spans, SPAN)
    before = doc_index(doc_lengths, positions - 1).reshape(spans, SPAN)[:, 0]
    span_shape = (spans, SPAN, HEADS, HEAD_DIM)
    query_rows = queries.reshape(span_shape)
    key_rows = keys_in.reshape(span_shape)
    value_rows = values_in.reshape(span_shape)
    decay_rows = log_decay.astype(jnp.float32).reshape(spans, SPAN, HEADS)
    inside, leading, factor, update = span_pass(
        query_rows, key_rows, value_rows, decay_rows, documents, before
    )
    prior_factor, prior_update, device_factor, device_update = prefix_states(factor, update)
    owner_factor, owner_update = (
        lax.all_to_all(
            device_factor.reshape(1, HEADS), "seq", split_axis=1, concat_axis=0, tiled=True
        ),
        lax.all_to_all(
            device_update.reshape(1, HEADS, HEAD_DIM, HEAD_DIM),
            "seq",
            split_axis=1,
            concat_axis=0,
            tiled=True,
        ),
    )
    entry_factor, entry_update, total_factor, total_update = prefix_states(
        owner_factor, owner_update
    )
    incoming_update = lax.all_to_all(
        entry_update, "seq", split_axis=0, concat_axis=1, tiled=True
    ).reshape(HEADS, HEAD_DIM, HEAD_DIM)
    states = prior_factor[:, :, None, None] * incoming_update[None] + prior_update
    mixed = with_state(query_rows, inside, leading, states).reshape(local_len, HEADS * HEAD_DIM)
    inverse_rms = lax.rsqrt(jnp.mean(mixed * mixed, axis=1, keepdims=True) + EPS)
    gated = (
        mixed * inverse_rms * norm_gain[None, :] * jax.nn.sigmoid(gate_logits.astype(jnp.float32))
    )
    return (gated.astype(jnp.bfloat16), total_update)


def solution(mesh):
    in_specs = (
        P(("grp", "seq"), None),
        P(("grp", "seq"), None),
        P(("grp", "seq"), None),
        P(("grp", "seq"), None),
        P(("grp", "seq"), None),
        P(),
        P("grp"),
    )
    out_specs = (P(("grp", "seq"), None), P(("grp", "seq"), None, None))
    return jax.shard_map(shards, mesh=mesh, in_specs=in_specs, out_specs=out_specs, check_vma=False)
```

profile of v0, /device:TPU:13, one launch (start us, length us, event | category | flops | bytes accessed | tf_op | source)
XLA Modules:
  0.0 327.3 jit_solution(16462266262842617301)
XLA Ops:
  0.7 0.8 reduce-window.8
  1.5 0.1 convert_reduce_fusion
  1.6 0.5 slice.150
  2.1 0.6 slice.147
  4.0 0.2 fusion.25
  4.1 0.2 multiply_reduce_fusion.1
  4.3 0.7 mul.191
  5.0 6.5 %all-to-all-start.1 = ((f32[1,16,4]{2,0,1:T(1,128)}), f32[1,16,4]{2,0,1:T(1,128)S(1)}, u32[]{:S(2)}, u32[]{:S(2)}) async-start(f32[1,16,4]{2,0,1:T(1,128)} %bitcast.18), calls=%async_computation.1 | async-start | bytes 16384 | tf_op jit(solution)/shard_map/all_to_all | solution.py:101
  11.6 6.4 %copy.65 = bf16[256,8192]{0,1:T(8,128)(2,1)} copy(bf16[256,8192]{1,0:T(8,128)(2,1)} %param.8) | data formatting | bytes 8388608 | tf_op jit(solution)/shard_map/reshape.12
  17.9 1.2 compare_convert_fusion.1
  19.2 0.1 multiply_bitcast_fusion.1
  19.3 6.7 %fusion.17 = f32[1,64,128,128]{3,2,0,1:T(8,128)} fusion(bf16[256,64,128]{0,2,1:T(8,128)(2,1)} %bitcast.85, f32[256,64]{0,1:T(8,128)S(1)} %get-tuple-element.32, bf16[256,8192]{1,0:T(8,128)(2,1)} %param.9), kind=kOutput, calls=%fused_computation.19 | convolution fusion | flops 543162368 | bytes 12648448 | tf_op jit(solution)/shard_map/while/body/eval_jaxpr/gjhd,gjhe->ghde/dot_general | solution.py:40
  26.0 6.0 %all-to-all-start = ((f32[1,64,128,128]{3,2,0,1:T(8,128)}), f32[1,64,128,128]{3,2,0,1:T(8,128)}, u32[]{:S(2)}, u32[]{:S(2)}) async-start(f32[1,64,128,128]{3,2,0,1:T(8,128)} %fusion.17), calls=%async_computation | async-start | bytes 8388608 | tf_op jit(solution)/shard_map/all_to_all | solution.py:104
  32.0 0.1 copy.56
  32.1 0.1 slice.120
  32.2 0.1 slice.124
  32.3 0.1 slice.119
  32.4 0.1 copy.58
  32.4 0.1 slice.126
  32.5 0.1 slice.130
  32.6 0.1 slice.125
  32.7 0.1 copy.60
  32.8 0.1 slice.132
  32.9 0.1 slice.136
  33.0 0.1 copy.57
  33.1 0.1 copy.59
  33.2 0.1 copy.61
  33.3 0.2 slice_reduce_fusion.2
  33.5 0.2 slice_reduce_fusion.1
  33.7 90.8 %all-to-all-done = f32[1,64,128,128]{3,2,0,1:T(8,128)} async-done(((f32[1,64,128,128]{3,2,0,1:T(8,128)}), f32[1,64,128,128]{3,2,0,1:T(8,128)}, u32[]{:S(2)}, u32[]{:S(2)}) %all-to-all-start) | async-done | bytes 4194336 | tf_op jit(solution)/shard_map/all_to_all | solution.py:104
  124.5 1.0 slice_bitcast_fusion
  125.4 2.5 slice_add_fusion.1
  127.9 0.7 slice.152
  128.7 0.2 slice_add_fusion.2
  128.8 0.1 slice_add_fusion.3
  128.9 0.1 slice_add_fusion.4
  129.0 0.8 pad_add_fusion
  129.9 0.1 fusion.28
  130.0 0.9 pad_maximum_fusion.2
  130.8 3.5 %pad.28 = f32[4,4,128,128]{3,2,1,0:T(8,128)S(1)} pad(f32[2,4,128,128]{3,2,1,0:T(8,128)} %pad_maximum_fusion.2, f32[]{:T(128)} %constant.28.clone.1), padding=0_1_1x0_0_0x0_0_0x0_0_0 | pad | bytes 1572868 | tf_op jit(solution)/shard_map/pad | solution.py:72
  134.3 5.8 %pad.29 = f32[4,4,128,128]{3,2,1,0:T(8,128)} pad(f32[2,4,128,128]{3,2,1,0:T(8,128)} %pad_add_fusion, f32[]{:T(128)} %constant.28.clone.1), padding=1_0_1x0_0_0x0_0_0x0_0_0 | pad | bytes 1572868 | tf_op jit(solution)/shard_map/pad | solution.py:72
  140.1 2.4 add.96
  142.5 1.3 fusion.21
  143.8 0.1 pad_maximum_fusion.1
  143.9 6.3 %pad.30 = f32[8,4,128,128]{3,2,1,0:T(8,128)} pad(f32[4,4,128,128]{3,2,1,0:T(8,128)S(1)} %pad_maximum_fusion.1, f32[]{:T(128)} %constant.28.clone.1), padding=0_1_1x0_0_0x0_0_0x0_0_0 | pad | bytes 3145732 | tf_op jit(solution)/shard_map/pad | solution.py:72
  150.2 6.4 %pad.31 = f32[8,4,128,128]{3,2,1,0:T(8,128)} pad(f32[4,4,128,128]{3,2,1,0:T(8,128)S(1)} %copy-done.4, f32[]{:T(128)} %constant.28.clone.1), padding=1_0_1x0_0_0x0_0_0x0_0_0 | pad | bytes 3145732 | tf_op jit(solution)/shard_map/pad | solution.py:72
  156.6 2.6 add.98
  159.2 0.2 copy-done.2
  159.4 0.6 copy-done.3
  160.1 1.8 fusion.20
  161.9 1.5 pad_maximum_fusion
  163.4 18.4 %pad.32 = f32[16,4,128,128]{3,2,1,0:T(8,128)} pad(f32[8,4,128,128]{3,2,1,0:T(8,128)} %pad_maximum_fusion, f32[]{:T(128)} %constant.28.clone.1), padding=0_1_1x0_0_0x0_0_0x0_0_0 | pad | bytes 6291460 | tf_op jit(solution)/shard_map/pad | solution.py:72
  181.8 12.0 %pad.33 = f32[16,4,128,128]{3,2,1,0:T(8,128)} pad(f32[8,4,128,128]{3,2,1,0:T(8,128)S(1)} %add.98, f32[]{:T(128)} %constant.28.clone.1), padding=1_0_1x0_0_0x0_0_0x0_0_0 | pad | bytes 6291460 | tf_op jit(solution)/shard_map/pad | solution.py:72
  193.8 4.0 %slice_add_fusion = f32[15,4,128,128]{3,2,1,0:T(8,128)S(1)} fusion(f32[16,4,128,128]{3,2,1,0:T(8,128)} %pad.33, f32[16,4,128,128]{3,2,1,0:T(8,128)} %pad.32), kind=kLoop, calls=%fused_computation.14 | loop fusion | flops 983040 | bytes 11796480 | tf_op jit(solution)/shard_map/add | solution.py:72
  197.8 2.5 concatenate.15
  200.2 4.9 %all-to-all-start.2 = ((f32[16,4,128,128]{3,2,1,0:T(8,128)}), f32[16,4,128,128]{3,2,1,0:T(8,128)}, u32[]{:S(2)}, u32[]{:S(2)}) async-start(f32[16,4,128,128]{3,2,1,0:T(8,128)} %concatenate.15), calls=%async_computation.2 | async-start | bytes 8388608 | tf_op jit(solution)/shard_map/all_to_all | solution.py:115
  205.1 0.1 fusion.26
  205.3 11.7 %fusion.2 = f32[64,256,128]{1,2,0:T(8,128)} fusion(bf16[256,64,128]{0,2,1:T(8,128)(2,1)} %bitcast.86, f32[64,256]{1,0:T(8,128)S(1)} %bitcast.88, pred[256,256]{1,0:T(8,128)(4,1)S(1)} %fusion.26, bf16[256,8192]{1,0:T(8,128)(2,1)} %param.9, bf16[256,8192]{1,0:T(8,128)(2,1)} %param.7), kind=kOutput, calls=%fused_computation.7 | convolution fusion | flops 2168455168 | bytes 21102592 | tf_op jit(solution)/shard_map/while/body/eval_jaxpr/ghij,gjhd->gihd/dot_general | solution.py:34
  217.0 12.0 %pad.62 = f32[15,4,128,128]{3,2,1,0:T(8,128)} pad(f32[8,4,128,128]{3,2,1,0:T(8,128)S(1)} %add.98, f32[]{:T(128)} %constant.28.clone.1), padding=0_0_1x0_0_0x0_0_0x0_0_0 | pad | bytes 6029316
  229.0 1.7 add_bitcast_fusion
  230.7 66.9 %all-to-all-done.2 = f32[16,4,128,128]{3,2,1,0:T(8,128)} async-done(((f32[16,4,128,128]{3,2,1,0:T(8,128)}), f32[16,4,128,128]{3,2,1,0:T(8,128)}, u32[]{:S(2)}, u32[]{:S(2)}) %all-to-all-start.2) | async-done | bytes 4194336 | tf_op jit(solution)/shard_map/all_to_all | solution.py:115
  297.6 13.6 %multiply_reduce_fusion = (f32[256]{0:T(256)S(1)}, f32[1,256,64,128]{1,3,2,0:T(8,128)}) fusion(f32[256,64]{0,1:T(8,128)S(1)} %get-tuple-element.44, f32[64,128,128]{2,1,0:T(8,128)} %bitcast.33, f32[64,256,128]{1,2,0:T(8,128)} %fusion.2, bf16[256,8192]{1,0:T(8,128)(2,1)} %param.7), kind=kOutput, calls=%fused_computation.4 | convolution fusion | flops 3229613824 | bytes 25232384 | tf_op jit(solution)/shard_map/nihd,nhde->nihe/dot_general | solution.py:79
  311.3 8.9 %copy.64 = f32[256,8192]{1,0:T(8,128)} copy(f32[256,8192]{0,1:T(8,128)} %bitcast.84) | data formatting | bytes 16777216 | tf_op jit(solution)/shard_map/reshape | solution.py:119
  320.2 7.2 %multiply_convert_fusion.1 = bf16[256,8192]{1,0:T(8,128)(2,1)} fusion(bf16[256,8192]{1,0:T(8,128)(2,1)} %param.11, f32[256,8192]{1,0:T(8,128)} %copy.64, f32[8192]{0:T(1024)S(1)} %copy-done.8, f32[256]{0:T(256)S(1)} %add_rsqrt_fusion), kind=kLoop, calls=%fused_computation.3 | loop fusion | flops 16777216 | bytes 16811008 | tf_op jit(solution)/shard_map/convert_element_type | solution.py:124
  (22 shorter events, 0.1 us)
Async XLA Ops:
  0.6 3.3 %copy-start = (bf16[256,64]{0,1:T(8,128)(2,1)S(1)}, bf16[256,64]{0,1:T(8,128)(2,1)}, u32[]{:S(2)}) copy-start(bf16[256,64]{0,1:T(8,128)(2,1)} %param.10) | copy-start | bytes 98308
  4.1 15.0 %copy-start.6 = (f32[256,64]{0,1:T(8,128)}, f32[256,64]{0,1:T(8,128)S(1)}, u32[]{:S(2)}) copy-start(f32[256,64]{0,1:T(8,128)S(1)} %fusion.25) | copy-start | bytes 196612
  5.0 20.9 %all-to-all-start.1 = ((f32[1,16,4]{2,0,1:T(1,128)}), f32[1,16,4]{2,0,1:T(1,128)S(1)}, u32[]{:S(2)}, u32[]{:S(2)}) async-start(f32[1,16,4]{2,0,1:T(1,128)} %bitcast.18), calls=%async_computation.1 | async-start | bytes 16384 | tf_op jit(solution)/shard_map/all_to_all | solution.py:101
  26.0 98.5 %all-to-all-start = ((f32[1,64,128,128]{3,2,0,1:T(8,128)}), f32[1,64,128,128]{3,2,0,1:T(8,128)}, u32[]{:S(2)}, u32[]{:S(2)}) async-start(f32[1,64,128,128]{3,2,0,1:T(8,128)} %fusion.17), calls=%async_computation | async-start | bytes 8388608 | tf_op jit(solution)/shard_map/all_to_all | solution.py:104
  140.1 3.7 %copy-start.5 = (f32[1,4,128,128]{3,2,1,0:T(8,128)S(1)}, f32[1,4,128,128]{3,2,1,0:T(8,128)}, u32[]{:S(2)}) copy-start(f32[1,4,128,128]{3,2,1,0:T(8,128)} %slice.152) | copy-start | bytes 786436
  143.8 6.4 %copy-start.4 = (f32[4,4,128,128]{3,2,1,0:T(8,128)S(1)}, f32[4,4,128,128]{3,2,1,0:T(8,128)}, u32[]{:S(2)}) copy-start(f32[4,4,128,128]{3,2,1,0:T(8,128)} %add.96) | copy-start | bytes 3145732
  156.6 2.9 copy-start.2
  156.6 3.5 %copy-start.3 = (f32[8,4,128,128]{3,2,1,0:T(8,128)S(1)}, f32[8,4,128,128]{3,2,1,0:T(8,128)}, u32[]{:S(2)}) copy-start(f32[8,4,128,128]{3,2,1,0:T(8,128)} %pad.31) | copy-start | bytes 6291460
  200.2 5.0 %copy-start.7 = (f32[256,64]{0,1:T(8,128)S(1)}, f32[256,64]{0,1:T(8,128)}, u32[]{:S(2)}) copy-start(f32[256,64]{0,1:T(8,128)} %copy-done.6) | copy-start | bytes 196612
  200.2 97.4 %all-to-all-start.2 = ((f32[16,4,128,128]{3,2,1,0:T(8,128)}), f32[16,4,128,128]{3,2,1,0:T(8,128)}, u32[]{:S(2)}, u32[]{:S(2)}) async-start(f32[16,4,128,128]{3,2,1,0:T(8,128)} %concatenate.15), calls=%async_computation.2 | async-start | bytes 8388608 | tf_op jit(solution)/shard_map/all_to_all | solution.py:115
  311.3 8.9 %copy-start.8 = (f32[8192]{0:T(1024)S(1)}, f32[8192]{0:T(1024)}, u32[]{:S(2)}) copy-start(f32[8192]{0:T(1024)} %param.12) | copy-start | bytes 98308
  320.2 7.2 %copy-start.1 = (bf16[256,64]{0,1:T(8,128)(2,1)S(1)}, bf16[256,64]{0,1:T(8,128)(2,1)}, u32[]{:S(2)}) copy-start(bf16[256,64]{0,1:T(8,128)(2,1)} %param.10) | copy-start | bytes 98308
where the time goes:
time: 330 us; the launch traced here: 327 us
  waiting for transfers between devices  158 us (48%)
  local copies, waits for them, and re-layouts  88.2 us (27%)
  matrix products  32.2 us (10%)
  other arithmetic  29.8 us (9%)
  starting transfers between devices  17.5 us (5%)
    all_to_all x1, waiting for transfers between devices, shards(): lax.all_to_all(device_update.reshape(1, HEADS, HEAD_DIM, HEAD_DIM), 'seq'...  90.8 us
    all_to_all x1, waiting for transfers between devices, shards(): lax.all_to_all(entry_update, 'seq', split_axis=0, concat_axis=1, tiled=True)  66.9 us
    pad x6, local copies, waits for them, and re-layouts, prefix_states(): lax.associative_scan(join_states, (factor, update), axis=0)  52.3 us
    dot_general x1, matrix products, with_state(): jnp.einsum('nihd,nhde->nihe', query_rows.astype(jnp.float32), states, pre...  13.6 us
    unnamed x19, local copies, waits for them, and re-layouts  12.9 us
    dot_general x1, matrix products, local_terms(): jnp.einsum('ghij,gjhd->gihd', weights, value_blk, preferred_element_type=...  11.7 us
    add x4, other arithmetic, prefix_states(): lax.associative_scan(join_states, (factor, update), axis=0)  9.85 us
    reshape x1, local copies, waits for them, and re-layouts, shards(): with_state(query_rows, inside, leading, states)  8.91 us
  transfers between devices with their start and end apart: 3, of which 2 were waited for; matrix products, arithmetic and copies ran while one was open for 13% of the time, Pallas kernels for 0%

commit v1 on v0

--- a/solution.py
+++ b/solution.py
@@ -112,8 +112,11 @@
     entry_factor, entry_update, total_factor, total_update = prefix_states(
         owner_factor, owner_update
     )
-    incoming_update = lax.all_to_all(
-        entry_update, "seq", split_axis=0, concat_axis=1, tiled=True
+    incoming_update = jnp.concatenate(
+        lax.all_to_all(
+            jnp.stack(jnp.split(entry_update, lax.axis_size("seq"), axis=0)), "seq", 0, 0
+        ),
+        axis=1,
     ).reshape(HEADS, HEAD_DIM, HEAD_DIM)
     states = prior_factor[:, :, None, None] * incoming_update[None] + prior_update
     mixed = with_state(query_rows, inside, leading, states).reshape(local_len, HEADS * HEAD_DIM)

time: 330 us -> 353 us (1.070)
  other arithmetic: 29.8 us -> 51.6 us
    unnamed x0 -> x14, other arithmetic: none -> 24.2 us
    add x4 -> x3, other arithmetic: 9.85 us -> 5.76 us  [prefix_states(): lax.associative_scan(join_states, (factor, update), axis=0)]
    pad x6, local copies, waits for them, and re-layouts: 52.3 us -> 56 us  [prefix_states(): lax.associative_scan(join_states, (factor, update), axis=0)]
    unnamed x19 -> x18, local copies, waits for them, and re-layouts: 12.9 us -> 13.5 us
  transfers between devices with their start and end apart: 3 -> 3, of which waited for: 2 -> 2; matrix products, arithmetic and copies ran while one was open for 13% -> 12% of each run, Pallas kernels for 0% -> 0%
where the time goes in v1:
time: 353 us; the launch traced here: 350 us
  waiting for transfers between devices  157 us (44%)
  local copies, waits for them, and re-layouts  89.3 us (25%)
  other arithmetic  51.6 us (15%)
  matrix products  32.2 us (9%)
  starting transfers between devices  17.4 us (5%)
    all_to_all x1, waiting for transfers between devices, shards(): lax.all_to_all(device_update.reshape(1, HEADS, HEAD_DIM, HEAD_DIM), 'seq'...  90.1 us
    all_to_all x1, waiting for transfers between devices, shards(): lax.all_to_all(jnp.stack(jnp.split(entry_update, lax.axis_size('seq'), ax...  67.1 us
    pad x6, local copies, waits for them, and re-layouts, prefix_states(): lax.associative_scan(join_states, (factor, update), axis=0)  56 us
    unnamed x14, other arithmetic  24.2 us
    dot_general x1, matrix products, with_state(): jnp.einsum('nihd,nhde->nihe', query_rows.astype(jnp.float32), states, pre...  13.6 us
    unnamed x18, local copies, waits for them, and re-layouts  13.5 us
    dot_general x1, matrix products, local_terms(): jnp.einsum('ghij,gjhd->gihd', weights, value_blk, preferred_element_type=...  11.7 us
    reshape x1, local copies, waits for them, and re-layouts, shards(): with_state(query_rows, inside, leading, states)  8.91 us
  transfers between devices with their start and end apart: 3, of which 2 were waited for; matrix products, arithmetic and copies ran while one was open for 12% of the time, Pallas kernels for 0%

profile of v1, /device:TPU:13, one launch (start us, length us, event | category | flops | bytes accessed | tf_op | source)
XLA Modules:
  0.0 349.8 jit_solution(724919590423064499)
XLA Ops:
  0.7 0.8 reduce-window.8
  1.6 0.7 slice.159
  2.2 0.5 slice.162
  4.0 0.2 fusion.40
  4.2 0.2 multiply_reduce_fusion.1
  4.4 0.7 mul.191
  5.1 6.5 %all-to-all-start.1 = ((f32[1,16,4]{2,0,1:T(1,128)}), f32[1,16,4]{2,0,1:T(1,128)S(1)}, u32[]{:S(2)}, u32[]{:S(2)}) async-start(f32[1,16,4]{2,0,1:T(1,128)} %bitcast.18), calls=%async_computation.1 | async-start | bytes 16384 | tf_op jit(solution)/shard_map/all_to_all | solution.py:101
  11.6 6.4 %copy.65 = bf16[256,8192]{0,1:T(8,128)(2,1)} copy(bf16[256,8192]{1,0:T(8,128)(2,1)} %param.8) | data formatting | bytes 8388608 | tf_op jit(solution)/shard_map/reshape.12
  18.0 1.2 compare_convert_fusion.1
  19.3 6.7 %fusion.17 = f32[1,64,128,128]{3,2,0,1:T(8,128)} fusion(bf16[256,64,128]{0,2,1:T(8,128)(2,1)} %bitcast.145, f32[256,64]{0,1:T(8,128)S(1)} %get-tuple-element.32, bf16[256,8192]{1,0:T(8,128)(2,1)} %param.9), kind=kOutput, calls=%fused_computation.18 | convolution fusion | flops 543162368 | bytes 12648448 | tf_op jit(solution)/shard_map/while/body/eval_jaxpr/gjhd,gjhe->ghde/dot_general | solution.py:40
  26.0 6.0 %all-to-all-start = ((f32[1,64,128,128]{3,2,0,1:T(8,128)}), f32[1,64,128,128]{3,2,0,1:T(8,128)}, u32[]{:S(2)}, u32[]{:S(2)}) async-start(f32[1,64,128,128]{3,2,0,1:T(8,128)} %fusion.17), calls=%async_computation | async-start | bytes 8388608 | tf_op jit(solution)/shard_map/all_to_all | solution.py:104
  32.1 0.7 broadcast_dynamic-update-slice_fusion
  32.9 0.1 slice.133
  33.0 0.1 slice.137
  33.1 0.1 slice.139
  33.4 0.1 slice.145
  33.7 0.1 slice.132
  34.1 0.2 slice_reduce_fusion.2
  34.3 0.2 slice_reduce_fusion.1
  34.5 90.1 %all-to-all-done = f32[1,64,128,128]{3,2,0,1:T(8,128)} async-done(((f32[1,64,128,128]{3,2,0,1:T(8,128)}), f32[1,64,128,128]{3,2,0,1:T(8,128)}, u32[]{:S(2)}, u32[]{:S(2)}) %all-to-all-start) | async-done | bytes 4194336 | tf_op jit(solution)/shard_map/all_to_all | solution.py:104
  124.5 2.5 slice_add_fusion
  127.0 0.2 slice_add_fusion.1
  127.2 0.1 slice_add_fusion.2
  127.4 0.8 pad_add_fusion
  128.3 0.1 fusion.43
  128.4 0.8 pad_maximum_fusion.2
  129.2 3.5 %pad.27 = f32[4,4,128,128]{3,2,1,0:T(8,128)S(1)} pad(f32[2,4,128,128]{3,2,1,0:T(8,128)} %pad_maximum_fusion.2, f32[]{:T(128)} %constant.28.clone.1), padding=0_1_1x0_0_0x0_0_0x0_0_0 | pad | bytes 1572868 | tf_op jit(solution)/shard_map/pad | solution.py:72
  132.7 5.7 %pad.28 = f32[4,4,128,128]{3,2,1,0:T(8,128)} pad(f32[2,4,128,128]{3,2,1,0:T(8,128)} %pad_add_fusion, f32[]{:T(128)} %constant.28.clone.1), padding=1_0_1x0_0_0x0_0_0x0_0_0 | pad | bytes 1572868 | tf_op jit(solution)/shard_map/pad | solution.py:72
  138.4 2.3 add.94
  140.8 10.1 %pad.30 = f32[8,4,128,128]{3,2,1,0:T(8,128)} pad(f32[4,4,128,128]{3,2,1,0:T(8,128)} %add.94, f32[]{:T(128)} %constant.28.clone.1), padding=1_0_1x0_0_0x0_0_0x0_0_0 | pad | bytes 3145732 | tf_op jit(solution)/shard_map/pad | solution.py:72
  150.9 1.3 fusion.21
  152.3 6.3 %pad.29 = f32[8,4,128,128]{3,2,1,0:T(8,128)} pad(f32[4,4,128,128]{3,2,1,0:T(8,128)S(1)} %pad_maximum_fusion.1, f32[]{:T(128)} %constant.28.clone.1), padding=0_1_1x0_0_0x0_0_0x0_0_0 | pad | bytes 3145732 | tf_op jit(solution)/shard_map/pad | solution.py:72
  158.6 2.6 add.96
  161.2 0.2 copy-done.2
  161.5 0.6 copy-done.3
  162.1 1.8 fusion.20
  163.9 1.0 slice_bitcast_fusion
  164.9 1.5 pad_maximum_fusion
  166.4 18.4 %pad.31 = f32[16,4,128,128]{3,2,1,0:T(8,128)} pad(f32[8,4,128,128]{3,2,1,0:T(8,128)} %pad_maximum_fusion, f32[]{:T(128)} %constant.28.clone.1), padding=0_1_1x0_0_0x0_0_0x0_0_0 | pad | bytes 6291460 | tf_op jit(solution)/shard_map/pad | solution.py:72
  184.8 12.0 %pad.32 = f32[16,4,128,128]{3,2,1,0:T(8,128)} pad(f32[8,4,128,128]{3,2,1,0:T(8,128)S(1)} %add.96, f32[]{:T(128)} %constant.28.clone.1), padding=1_0_1x0_0_0x0_0_0x0_0_0 | pad | bytes 6291460 | tf_op jit(solution)/shard_map/pad | solution.py:72
  196.8 1.9 fusion.39
  198.7 1.8 fusion.38
  200.4 1.8 fusion.37
  202.2 1.8 fusion.36
  203.9 1.8 fusion.35
  205.7 1.8 fusion.34
  207.5 1.7 fusion.33
  209.2 1.7 fusion.32
  210.8 1.7 fusion.31
  212.5 1.7 fusion.30
  214.2 1.7 fusion.29
  215.9 1.7 fusion.28
  217.6 1.7 fusion.27
  219.3 1.7 fusion.26
  221.0 1.7 fusion.25
  222.6 4.9 %all-to-all-start.2 = ((f32[16,1,4,128,128]{4,3,2,1,0:T(8,128)}), f32[16,1,4,128,128]{4,3,2,1,0:T(8,128)}, u32[]{:S(2)}, u32[]{:S(2)}) async-start(f32[16,1,4,128,128]{4,3,2,1,0:T(8,128)} %fusion.25), calls=%async_computation.2 | async-start | bytes 8388608 | tf_op jit(solution)/shard_map/all_to_all | solution.py:116
  227.6 0.1 fusion.41
  227.7 11.7 %fusion.2 = f32[64,256,128]{1,2,0:T(8,128)} fusion(bf16[256,64,128]{0,2,1:T(8,128)(2,1)} %bitcast.146, f32[64,256]{1,0:T(8,128)S(1)} %bitcast.148, pred[256,256]{1,0:T(8,128)(4,1)S(1)} %fusion.41, bf16[256,8192]{1,0:T(8,128)(2,1)} %param.9, bf16[256,8192]{1,0:T(8,128)(2,1)} %param.7), kind=kOutput, calls=%fused_computation.7 | convolution fusion | flops 2168455168 | bytes 21102592 | tf_op jit(solution)/shard_map/while/body/eval_jaxpr/ghij,gjhd->gihd/dot_general | solution.py:34
  239.4 11.9 %pad.61 = f32[15,4,128,128]{3,2,1,0:T(8,128)} pad(f32[8,4,128,128]{3,2,1,0:T(8,128)S(1)} %add.96, f32[]{:T(128)} %constant.28.clone.1), padding=0_0_1x0_0_0x0_0_0x0_0_0 | pad | bytes 6029316
  251.3 1.7 add_bitcast_fusion.15
  252.9 67.1 %all-to-all-done.2 = f32[16,1,4,128,128]{4,3,2,1,0:T(8,128)} async-done(((f32[16,1,4,128,128]{4,3,2,1,0:T(8,128)}), f32[16,1,4,128,128]{4,3,2,1,0:T(8,128)}, u32[]{:S(2)}, u32[]{:S(2)}) %all-to-all-start.2) | async-done | bytes 4194336 | tf_op jit(solution)/shard_map/all_to_all | solution.py:116
  320.0 13.6 %multiply_reduce_fusion = (f32[256]{0:T(256)S(1)}, f32[1,256,64,128]{1,3,2,0:T(8,128)}) fusion(f32[256,64]{0,1:T(8,128)S(1)} %get-tuple-element.44, f32[64,128,128]{2,1,0:T(8,128)} %bitcast.48, f32[64,256,128]{1,2,0:T(8,128)} %fusion.2, bf16[256,8192]{1,0:T(8,128)(2,1)} %param.7), kind=kOutput, calls=%fused_computation.4 | convolution fusion | flops 3229613824 | bytes 25232384 | tf_op jit(solution)/shard_map/nihd,nhde->nihe/dot_general | solution.py:79
  333.7 8.9 %copy.64 = f32[256,8192]{1,0:T(8,128)} copy(f32[256,8192]{0,1:T(8,128)} %bitcast.144) | data formatting | bytes 16777216 | tf_op jit(solution)/shard_map/reshape | solution.py:122
  342.6 7.2 %multiply_convert_fusion.1 = bf16[256,8192]{1,0:T(8,128)(2,1)} fusion(bf16[256,8192]{1,0:T(8,128)(2,1)} %param.11, f32[256,8192]{1,0:T(8,128)} %copy.64, f32[8192]{0:T(1024)S(1)} %copy-done.7, f32[256]{0:T(256)S(1)} %add_rsqrt_fusion), kind=kLoop, calls=%fused_computation.3 | loop fusion | flops 16777216 | bytes 16811008 | tf_op jit(solution)/shard_map/convert_element_type | solution.py:127
  (34 shorter events, 1.2 us)
Async XLA Ops:
  0.6 3.4 copy-start
  4.2 15.1 %copy-start.5 = (f32[256,64]{0,1:T(8,128)}, f32[256,64]{0,1:T(8,128)S(1)}, u32[]{:S(2)}) copy-start(f32[256,64]{0,1:T(8,128)S(1)} %fusion.40) | copy-start | bytes 196612
  5.1 20.9 %all-to-all-start.1 = ((f32[1,16,4]{2,0,1:T(1,128)}), f32[1,16,4]{2,0,1:T(1,128)S(1)}, u32[]{:S(2)}, u32[]{:S(2)}) async-start(f32[1,16,4]{2,0,1:T(1,128)} %bitcast.18), calls=%async_computation.1 | async-start | bytes 16384 | tf_op jit(solution)/shard_map/all_to_all | solution.py:101
  26.0 98.5 %all-to-all-start = ((f32[1,64,128,128]{3,2,0,1:T(8,128)}), f32[1,64,128,128]{3,2,0,1:T(8,128)}, u32[]{:S(2)}, u32[]{:S(2)}) async-start(f32[1,64,128,128]{3,2,0,1:T(8,128)} %fusion.17), calls=%async_computation | async-start | bytes 8388608 | tf_op jit(solution)/shard_map/all_to_all | solution.py:104
  158.6 2.9 copy-start.2
  158.6 3.5 copy-start.3
  196.7 10.7 %copy-start.4 = (f32[16,4,128,128]{3,2,1,0:T(8,128)S(1)}, f32[16,4,128,128]{3,2,1,0:T(8,128)}, u32[]{:S(2)}) copy-start(f32[16,4,128,128]{3,2,1,0:T(8,128)} %pad.31) | copy-start | bytes 12582916
  222.6 5.0 %copy-start.6 = (f32[256,64]{0,1:T(8,128)S(1)}, f32[256,64]{0,1:T(8,128)}, u32[]{:S(2)}) copy-start(f32[256,64]{0,1:T(8,128)} %copy-done.5) | copy-start | bytes 196612
  222.6 97.4 %all-to-all-start.2 = ((f32[16,1,4,128,128]{4,3,2,1,0:T(8,128)}), f32[16,1,4,128,128]{4,3,2,1,0:T(8,128)}, u32[]{:S(2)}, u32[]{:S(2)}) async-start(f32[16,1,4,128,128]{4,3,2,1,0:T(8,128)} %fusion.25), calls=%async_computation.2 | async-start | bytes 8388608 | tf_op jit(solution)/shard_map/all_to_all | solution.py:116
  333.7 8.9 %copy-start.7 = (f32[8192]{0:T(1024)S(1)}, f32[8192]{0:T(1024)}, u32[]{:S(2)}) copy-start(f32[8192]{0:T(1024)} %param.12) | copy-start | bytes 98308
  342.6 7.2 %copy-start.1 = (bf16[256,64]{0,1:T(8,128)(2,1)S(1)}, bf16[256,64]{0,1:T(8,128)(2,1)}, u32[]{:S(2)}) copy-start(bf16[256,64]{0,1:T(8,128)(2,1)} %param.10) | copy-start | bytes 98308
